TPU v7x, 32 devices: a whole 2x2x4 slice. The times are simulated.
32 devices in a mesh: gz: 8 (over z, x), gy: 4 (over y, core).
Axes of the slice: x: 2, y: 2, z: 4, core: 2. Of those that a mesh axis runs over, the one named last changes fastest.
Arguments:
- fields: float32 [2, 256, 256, 128], P(None, 'gz', 'gy'), may hold values from -7 to 8
- residual: float32 [2, 256, 256, 128], P(None, 'gz', 'gy'), may hold values from -14 to 14
- past_fields: float32 [20, 2, 256, 256, 128], P(None, None, 'gz', 'gy'), may hold values from -7 to 8
- past_residuals: float32 [20, 2, 256, 256, 128], P(None, None, 'gz', 'gy'), may hold values from -14 to 14
Outputs:
- new_fields: float32 [2, 256, 256, 128], P(None, 'gz', 'gy')
- summary: float32 [3], replicated
All inputs are finite; a program needn't handle non-finite values.
Results may differ from a plain program's by a relative error of at most 0.0003.
Values sent between devices are 32-bit elements; how exact they have to be, the bound alone decides.
A program may use at most 192 MiB of HBM per device.

v0:
```python
import math

import jax
import jax.numpy as jnp
from jax import lax
from jax.sharding import PartitionSpec as P

CHI_N = 20.0
RIDGE = 0.01
STEP_LOCAL = 0.1
EXACT = lax.Precision.HIGHEST


def kernel_total(length):
    decay_len = length / 4.0
    offsets = lax.iota(jnp.int32, length).astype(jnp.float32)
    return jnp.sum(jnp.cosh((0.5 * length - offsets) / decay_len))


def kernel_rows(row_first, row_count, col_first, col_count, length):
    decay_len = length / 4.0
    row_index = row_first + lax.iota(jnp.int32, row_count)[:, None]
    col_index = col_first + lax.iota(jnp.int32, col_count)[None, :]
    lag = jnp.mod(row_index - col_index, length).astype(jnp.float32)
    return jnp.cosh((0.5 * length - lag) / decay_len) / kernel_total(length)


def end_moments(first, count, length):
    decay_len = length / 4.0
    place = (first + lax.iota(jnp.int32, count)).astype(jnp.float32) / decay_len
    return jnp.stack([jnp.exp(place), jnp.exp(-place)])


def far_weights(first, count, own_block, blocks, length):
    decay_len = length / 4.0
    place = (first + lax.iota(jnp.int32, count)).astype(jnp.float32) / decay_len
    block_index = lax.iota(jnp.int32, blocks)
    below = block_index < own_block
    above = block_index > own_block
    wide = math.exp(0.5 * length / decay_len)
    rising = jnp.where(below, wide, jnp.where(above, 1.0 / wide, 0.0))
    falling = jnp.where(below, 1.0 / wide, jnp.where(above, wide, 0.0))
    factor = 0.5 / kernel_total(length)
    weight_rising = factor * jnp.exp(-place)[:, None] * rising[None, :]
    weight_falling = factor * jnp.exp(place)[:, None] * falling[None, :]
    return jnp.stack([weight_rising, weight_falling], axis=2).reshape(count, 2 * blocks)


def shards(fields, residual, past_fields, past_residuals):
    history = past_residuals.shape[0]
    species, height_cells, width_cells, line_cells = residual.shape
    height_total = height_cells * lax.axis_size("gz")
    width_total = width_cells * lax.axis_size("gy")
    cell_total = height_total * width_total * line_cells
    flat_residual = residual.reshape(-1)
    past_rows = past_residuals.reshape(history, -1)
    deltas = flat_residual[None, :] - past_rows
    gram_local = jnp.dot(deltas, deltas.T, precision=EXACT, preferred_element_type=jnp.float32)
    intersect_local = jnp.dot(
        deltas, flat_residual, precision=EXACT, preferred_element_type=jnp.float32
    )
    residual_square = jnp.sum(residual * residual)
    field_square = jnp.sum(fields * fields)
    gram_matrix, intersect = lax.psum((gram_local, intersect_local), ("gz", "gy"))
    diagonal_shift = RIDGE * jnp.trace(gram_matrix) / history + 1.0
    system = gram_matrix + diagonal_shift * jnp.eye(history, dtype=jnp.float32)
    factor = jnp.linalg.cholesky(system)
    forward = lax.linalg.triangular_solve(factor, intersect[:, None], left_side=True, lower=True)
    coeffs = lax.linalg.triangular_solve(
        factor, forward, left_side=True, lower=True, transpose_a=True
    )[:, 0]
    remain_weight = 1.0 - jnp.sum(coeffs)
    field_mixed = remain_weight * fields + jnp.dot(
        coeffs,
        past_fields.reshape(history, -1),
        precision=EXACT,
        preferred_element_type=jnp.float32,
    ).reshape(fields.shape)
    residual_mixed = remain_weight * residual + jnp.dot(
        coeffs, past_rows, precision=EXACT, preferred_element_type=jnp.float32
    ).reshape(residual.shape)
    height_first = lax.axis_index("gz") * height_cells
    width_first = lax.axis_index("gy") * width_cells
    moments = jnp.einsum(
        "ab,sbyx->sayx",
        end_moments(height_first, height_cells, height_total),
        residual_mixed,
        precision=EXACT,
    )
    every_end = lax.all_gather(moments, "gz", axis=1, tiled=True)
    near = jnp.einsum(
        "ab,sbyx->sayx",
        kernel_rows(height_first, height_cells, height_first, height_cells, height_total),
        residual_mixed,
        precision=EXACT,
    )
    far = jnp.einsum(
        "ab,sbyx->sayx",
        far_weights(
            height_first, height_cells, lax.axis_index("gz"), lax.axis_size("gz"), height_total
        ),
        every_end,
        precision=EXACT,
    )
    smoothed_half = near + far
    portion = lax.all_gather(smoothed_half, "gy", axis=2, tiled=True)
    kernel = kernel_rows(width_first, width_cells, jnp.int32(0), portion.shape[2], width_total)
    smoothed = jnp.zeros_like(smoothed_half) + jnp.einsum(
        "ab,szbx->szax", kernel, portion, precision=EXACT
    )
    new_fields = field_mixed + STEP_LOCAL * residual_mixed + smoothed
    split_field = new_fields[0] - new_fields[1]
    sum_field = new_fields[0] + new_fields[1]
    energy_local = jnp.sum(split_field * split_field / (4.0 * CHI_N) - 0.5 * sum_field)
    peak_local = jnp.max(jnp.abs(residual_mixed))
    energy_total, residual_total, field_total = lax.psum(
        (energy_local, residual_square, field_square), ("gz", "gy")
    )
    largest = lax.pmax(peak_local, ("gz", "gy"))
    relative = jnp.sqrt(residual_total / (field_total + 1.0))
    summary = jnp.stack([energy_total / cell_total, relative, largest])
    return (new_fields, summary)


def solution(mesh):
    placed = (
        P(None, "gz", "gy", None),
        P(None, "gz", "gy", None),
        P(None, None, "gz", "gy", None),
        P(None, None, "gz", "gy", None),
    )
    return jax.shard_map(
        shards,
        mesh=mesh,
        in_specs=placed,
        out_specs=(P(None, "gz", "gy", None), P()),
        check_vma=False,
    )
```

profile of v0, /device:TPU:0, one launch (start us, length us, event | category | flops | bytes accessed | tf_op | source)
XLA Modules:
  0.0 577.8 jit_solution(16843497883057855397)
XLA Ops:
  7.2 32.5 %broadcast_subtract_fusion = f32[20,2,32,64,128]{4,3,2,1,0:T(8,128)} fusion(f32[20,2,32,64,128]{4,3,2,1,0:T(8,128)} %param.7, f32[2,32,64,128]{3,2,1,0:T(8,128)} %param.5), kind=kLoop, calls=%fused_computation.8 | loop fusion | flops 10485760 | bytes 85983232 | tf_op jit(solution)/shard_map/sub | solution.py:57
  39.8 110.5 %fusion.21 = f32[20,20]{1,0:T(8,128)S(1)} fusion(f32[20,2,32,64,128]{4,3,2,1,0:T(8,128)} %broadcast_subtract_fusion), kind=kOutput, calls=%fused_computation.22 | convolution fusion | flops 2516582400 | bytes 41944640 | tf_op jit(solution)/shard_map/dot_general | solution.py:58
  150.2 75.0 %fusion.24 = f32[20]{0:T(128)S(1)} fusion(f32[2,32,64,128,1]{3,4,2,1,0:T(1,128)S(1)} %bitcast.108, f32[20,2,32,64,128]{4,3,2,1,0:T(8,128)} %broadcast_subtract_fusion), kind=kOutput, calls=%fused_computation.24 | convolution fusion | flops 125829120 | bytes 44040272 | tf_op jit(solution)/shard_map/dot_general | solution.py:59
  225.2 42.1 %all-reduce.1 = (f32[20,20]{1,0:T(8,128)S(1)}, f32[20]{0:T(128)S(1)}) all-reduce(f32[20,20]{1,0:T(8,128)S(1)} %fusion.21, f32[20]{0:T(128)S(1)} %fusion.24), channel_id=1, replica_groups=mesh['gz'=8,'gy'=4] {'gz','gy'}, use_global_device_ids=true, to_apply=%region_0.0 | all-reduce | flops 420 | bytes 3360 | tf_op jit(solution)/shard_map/psum | solution.py:64
  268.7 1.8 cholesky.17
  271.2 0.6 fusion.69
  271.9 1.5 custom-call.8
  273.6 0.8 bitcast_reduce_fusion
  275.0 74.0 %fusion.4 = f32[1,2,32,64,128]{4,0,3,2,1:T(1,128)S(1)} fusion(f32[2,32,64,128,20]{3,2,1,0,4:T(8,128)} %bitcast.106, f32[1,20]{1,0:T(1,128)S(1)} %get-tuple-element.11), kind=kOutput, calls=%fused_computation.4 | convolution fusion | flops 125829120 | bytes 44040272 | tf_op jit(solution)/shard_map/dot_general | solution.py:79
  349.0 1.3 abs_reduce_fusion
  350.3 2.4 fusion.18
  352.7 0.7 copy.17
  353.4 0.7 add_reduce_fusion
  355.0 38.6 %all-gather.3.cloned.1.call-done = f32[2,16,64,128]{3,2,0,1:T(8,128)} async-done(((f32[2,2,64,128]{3,2,0,1:T(8,128)}), f32[2,16,64,128]{3,2,0,1:T(8,128)}) %all-gather.3.cloned.1.call-update) | async-done | bytes 1048592 | tf_op jit(solution)/shard_map/all_gather | solution.py:90
  393.6 3.5 fusion.27
  397.1 5.3 add_bitcast_fusion
  402.5 39.2 %pmax.7 = f32[1]{0:T(128)} all-reduce(f32[1]{0:T(128)} %bitcast.37), channel_id=1, replica_groups=mesh['gz'=8,'gy'=4] {'gz','gy'}, use_global_device_ids=true, to_apply=%region_14.15 | all-reduce | flops 1 | bytes 8 | tf_op jit(solution)/shard_map/pmax | solution.py:119
  441.7 2.7 multiply_reduce_fusion
  444.4 63.8 %fusion.6 = f32[1,2,32,64,128]{4,0,3,2,1:T(1,128)} fusion(f32[2,32,64,128,20]{3,2,1,0,4:T(8,128)} %bitcast.107, f32[1,20]{1,0:T(1,128)S(1)} %get-tuple-element.11), kind=kOutput, calls=%fused_computation.6 | convolution fusion | flops 125829120 | bytes 44040272 | tf_op jit(solution)/shard_map/dot_general | solution.py:73
  508.2 15.2 %bitcast_add_fusion = f32[2,32,64,128]{3,2,1,0:T(8,128)S(1)} fusion(f32[2,32,64,128]{3,2,1,0:T(8,128)S(1)} %get-tuple-element.8, f32[2,32,64,128]{3,2,1,0:T(8,128)} %bitcast.109, f32[2,32,64,128]{3,2,1,0:T(8,128)} %param.4, f32[2,32,256,128]{3,1,2,0:T(8,128)} %all-gather.5.cloned.1.call-done, f32[]{:T(128)S(6)} %sub.67, f32[]{:T(128)} %add_reduce_fusion, ...), kind=kOutput, calls=%fused_computation.11 | convolution fusion | flops 1613545472 | bytes 16777480 | tf_op jit(solution)/shard_map/ab,szbx->szax/dot_general | solution.py:108
  523.5 1.3 copy-done.2
  524.8 0.9 subtract_reduce_fusion
  525.7 41.7 %all-reduce = (f32[]{:T(128)}, f32[]{:T(128)}, f32[]{:T(128)}) all-reduce(f32[]{:T(128)} %get-tuple-element.9, f32[]{:T(128)} %multiply_reduce_fusion, f32[]{:T(128)} %subtract_reduce_fusion), channel_id=1, replica_groups=mesh['gz'=8,'gy'=4] {'gz','gy'}, use_global_device_ids=true, to_apply=%region_10.11 | all-reduce | flops 3 | bytes 24 | tf_op jit(solution)/shard_map/psum | solution.py:116
  569.4 1.1 pad_maximum_fusion.1
  (25 shorter events, 1.9 us)
Async XLA Ops:
  7.2 386.5 %all-gather.3.cloned.1.call-start = ((), (), s32[]{:S(2)}) async-start(), calls=%async_computation | async-start | bytes 1179648 | tf_op jit(solution)/shard_map/all_gather | solution.py:90
  39.7 110.5 %copy-start = (f32[2,32,64,128]{3,2,1,0:T(8,128)S(1)}, f32[2,32,64,128]{3,2,1,0:T(8,128)}, u32[]{:S(2)}) copy-start(f32[2,32,64,128]{3,2,1,0:T(8,128)} %param.5) | copy-start | bytes 6291460
  275.0 74.0 %copy-start.1 = (f32[2,32,64,128]{3,2,1,0:T(8,128)S(1)}, f32[2,32,64,128]{3,2,1,0:T(8,128)}, u32[]{:S(2)}) copy-start(f32[2,32,64,128]{3,2,1,0:T(8,128)} %param.5) | copy-start | bytes 6291460
  353.4 154.9 %all-gather.5.cloned.1.call-start = ((), (), s32[]{:S(2)}) async-start(), calls=%async_computation.1 | async-start | bytes 10485760 | tf_op jit(solution)/shard_map/all_gather | solution.py:106
  523.4 1.3 copy-start.2
Sparse Core Ops, SparseCore 0:
  353.5 40.0 all-gather.2
  402.6 57.8 all-gather.4
where the time goes:
time: 588 us; the launch traced here: 578 us
  matrix products  351 us (60%)
  blocking collectives  123 us (21%)
  other arithmetic  44.7 us (8%)
  waiting for transfers between devices  38.7 us (7%)
  between operations  18.6 us (3%)
    dot_general x1, matrix products, shards(): jnp.dot(deltas, deltas.T, precision=EXACT, preferred_element_type=jnp.flo...  110 us
    dot_general x1, matrix products, shards(): jnp.dot(deltas, flat_residual, precision=EXACT, preferred_element_type=jn...  75 us
    dot_general x1, matrix products, shards(): jnp.dot(coeffs, past_rows, precision=EXACT, preferred_element_type=jnp.fl...  74 us
    dot_general x1, matrix products, shards(): jnp.dot(coeffs, past_fields.reshape(history, -1), precision=EXACT, prefer...  63.8 us
    psum x1, blocking collectives, shards(): lax.psum((gram_local, intersect_local), ('gz', 'gy'))  42.1 us
    psum x1, blocking collectives, shards(): lax.psum((energy_local, residual_square, field_square), ('gz', 'gy'))  41.7 us
    pmax x1, blocking collectives, shards(): largest = lax.pmax(peak_local, ('gz', 'gy'))  39.2 us
    all_gather x1, waiting for transfers between devices, shards(): every_end = lax.all_gather(moments, 'gz', axis=1, tiled=True)  38.6 us
  transfers between devices with their start and end apart: 2, of which 1 were waited for; matrix products, arithmetic and copies ran while one was open for 12% of the time, Pallas kernels for 0%

commit v1 on v0

v1 whole, which is shorter than its diff:
```python
import functools
import math

import jax
import jax.numpy as jnp
import numpy as np
from jax import lax
from jax.experimental import pallas as pl
from jax.experimental.pallas import tpu as pltpu
from jax.sharding import PartitionSpec as P

CHI_N = 20.0
RIDGE = 0.01
STEP_LOCAL = 0.1
EXACT = lax.Precision.HIGHEST
NT = (((1,), (1,)), ((), ()))


def params(count):
    return pltpu.CompilerParams(
        dimension_semantics=("arbitrary",) * count, vmem_limit_bytes=56 * 1024 * 1024
    )


def gram_kernel(history, past_ref, res_ref, field_ref, out_ref, high, low, acc, square):
    step = pl.program_id(0)

    @pl.when(step == 0)
    def _():
        acc[...] = jnp.zeros_like(acc)
        square[...] = jnp.zeros_like(square)

    rows = res_ref.shape[0]
    used = 8 * history
    size = high.shape[0]
    for g in range(rows // 8):
        part = pl.ds(8 * g, 8)
        lanes = pl.ds(128 * g, 128)
        current = res_ref[part, :]
        delta = (current[None] - past_ref[:, part, :]).reshape(used, 128)
        tail = jnp.concatenate([current, jnp.zeros((size - used - 8, 128), jnp.float32)], axis=0)
        for first, value in ((0, delta), (used, tail)):
            head = value.astype(jnp.bfloat16)
            rest = (value - head.astype(jnp.float32)).astype(jnp.bfloat16)
            high[pl.ds(first, value.shape[0]), lanes] = head
            low[pl.ds(first, value.shape[0]), lanes] = rest
    hi, lo = high[...], low[...]
    acc[0] += lax.dot_general(hi, hi, NT, preferred_element_type=jnp.float32)
    acc[1] += lax.dot_general(hi, lo, NT, preferred_element_type=jnp.float32)
    field = field_ref[...]
    square[...] += jnp.sum((field * field).reshape(rows // 8, 8, 128), axis=0)

    @pl.when(step == pl.num_programs(0) - 1)
    def _():
        same = lax.broadcasted_iota(jnp.int32, (size, size), 0) % 8 == (
            lax.broadcasted_iota(jnp.int32, (size, size), 1) % 8
        )
        pick_rows = (
            lax.broadcasted_iota(jnp.int32, (24, size), 1) // 8
            == lax.broadcasted_iota(jnp.int32, (24, size), 0)
        ).astype(jnp.float32)
        pick_cols = (
            lax.broadcasted_iota(jnp.int32, (128, size), 1) // 8
            == lax.broadcasted_iota(jnp.int32, (128, size), 0)
        ).astype(jnp.float32)

        def fold(a, b, value):
            inner = jnp.dot(a, jnp.where(same, value, 0.0), precision=EXACT, preferred_element_type=jnp.float32)
            return lax.dot_general(inner, b, NT, precision=EXACT, preferred_element_type=jnp.float32)

        cross = acc[1]
        out_ref[pl.ds(0, 24), :] = fold(pick_rows, pick_cols, acc[0] + cross + cross.T)
        out_ref[pl.ds(24, 8), :] = square[...]


def solve(history, parts_ref, coeff_ref, stats_ref):
    total = parts_ref[0]
    for k in range(1, parts_ref.shape[0]):
        total = total + parts_ref[k]
    matrix = total[0:24]
    field_square = jnp.sum(jnp.sum(total[24:32], axis=0, keepdims=True), axis=1, keepdims=True)
    residual_square = matrix[history : history + 1, history : history + 1]
    row = lax.broadcasted_iota(jnp.int32, (24, 128), 0)
    col = lax.broadcasted_iota(jnp.int32, (24, 128), 1)
    diagonal = (row == col) & (row < history)
    trace = jnp.sum(
        jnp.sum(jnp.where(diagonal, matrix, 0.0), axis=0, keepdims=True), axis=1, keepdims=True
    )
    shift = RIDGE * trace / history + 1.0
    matrix = jnp.where(row < history, matrix + jnp.where(diagonal, shift, 0.0), 0.0)
    for k in range(history):
        pivot = matrix[k : k + 1, :]
        scaled = pivot / matrix[k : k + 1, k : k + 1]
        column = matrix[:, k : k + 1]
        matrix = jnp.where(row == k, scaled, matrix - column * scaled)
    coeffs = jnp.broadcast_to(matrix[:, history : history + 1], (24, 128))
    remain = 1.0 - jnp.sum(coeffs, axis=0, keepdims=True)
    coeff_ref[...] = jnp.where(row == history, remain, coeffs)
    relative = jnp.sqrt(residual_square / (field_square + 1.0))
    stats_ref[pl.ds(0, 8), :] = jnp.zeros((8, 128), jnp.float32)
    stats_ref[pl.ds(8, 8), :] = jnp.broadcast_to(relative, (8, 128))


def mix_kernel(
    history, decay, parts_ref, pf_ref, pr_ref, field_ref, res_ref, base_ref, mixed_ref, ends_ref, stats_ref, coeff
):
    species, step = pl.program_id(0), pl.program_id(1)

    @pl.when((species == 0) & (step == 0))
    def _():
        solve(history, parts_ref, coeff, stats_ref)

    @pl.when(step == 0)
    def _():
        ends_ref[...] = jnp.zeros_like(ends_ref)

    planes, rows = res_ref.shape[1], res_ref.shape[2]
    peak = stats_ref[pl.ds(0, 8), :]
    weights = [coeff[pl.ds(i, 1), :] for i in range(history + 1)]
    for z in range(planes):
        place = jnp.full((1, 128), step * planes + z, jnp.int32).astype(jnp.float32)
        back = jnp.exp(-place * decay)
        for g in range(rows // 8):
            part = pl.ds(8 * g, 8)
            mixed = weights[history] * res_ref[0, z, part, :]
            field = weights[history] * field_ref[0, z, part, :]
            for i in range(history):
                mixed = mixed + weights[i] * pr_ref[i, 0, z, part, :]
                field = field + weights[i] * pf_ref[i, 0, z, part, :]
            mixed_ref[0, z, part, :] = mixed
            base_ref[0, z, part, :] = field + STEP_LOCAL * mixed
            peak = jnp.maximum(peak, jnp.abs(mixed))
            ends_ref[0, 0, part, :] = ends_ref[0, 0, part, :] * math.exp(-decay) + mixed
            ends_ref[0, 1, part, :] += back * mixed
    stats_ref[pl.ds(0, 8), :] = peak


def smooth_kernel(decay, weight_ref, ends_ref, taps_ref, mixed_ref, base_ref, out_ref, tops_ref, work):
    planes, rows = mixed_ref.shape[1], mixed_ref.shape[2]
    ratio = math.exp(-decay)
    blocks = ends_ref.shape[0]

    def carried(side):
        total = weight_ref[side, 0] * ends_ref[0, 0, side]
        for k in range(1, blocks):
            total = total + weight_ref[side, k] * ends_ref[k, 0, side]
        return total

    carry = carried(0)
    for z in range(planes):
        carry = carry * ratio + mixed_ref[0, z]
        work[z] = carry
    carry = carried(1)
    taps = taps_ref[...]
    for z in range(planes - 1, -1, -1):
        plane = work[z] + ratio * carry
        carry = carry * ratio + mixed_ref[0, z]
        result = jnp.dot(taps, plane, precision=EXACT, preferred_element_type=jnp.float32)
        out_ref[0, z] = base_ref[0, z] + result[0:rows]
        tops_ref[0, 0, pl.ds(z, 1), :] = result[rows : rows + 1]
        tops_ref[0, 1, pl.ds(z, 1), :] = result[rows + 1 : rows + 2]


def finish_kernel(decay, weight_ref, tops_ref, part_ref, out_ref, energy_ref):
    step = pl.program_id(0)

    @pl.when(step == 0)
    def _():
        energy_ref[...] = jnp.zeros_like(energy_ref)

    planes, rows = part_ref.shape[1], part_ref.shape[2]
    blocks = tops_ref.shape[0]
    place = lax.broadcasted_iota(jnp.int32, (rows, 128), 0).astype(jnp.float32)
    down = jnp.exp(-(place + 1.0) * decay)
    up = jnp.exp(-(rows - place) * decay)
    carry = []
    for s in range(2):
        pair = []
        for side in range(2):
            total = weight_ref[side, 0] * tops_ref[0, s, side]
            for k in range(1, blocks):
                total = total + weight_ref[side, k] * tops_ref[k, s, side]
            pair.append(total)
        carry.append(pair)
    energy = energy_ref[...]
    for z in range(planes):
        new = []
        for s in range(2):
            value = (
                part_ref[s, z]
                + down * carry[s][0][z : z + 1, :]
                + up * carry[s][1][z : z + 1, :]
            )
            out_ref[s, z] = value
            new.append(value)
        split = new[0] - new[1]
        term = split * split / (4.0 * CHI_N) - 0.5 * (new[0] + new[1])
        energy = energy + jnp.sum(term.reshape(rows // 8, 8, 128), axis=0)
    energy_ref[...] = energy


def carry_weights(axis, cells, total):
    blocks = lax.axis_size(axis)
    me = lax.axis_index(axis)
    step = 4.0 * cells / total
    other = lax.iota(jnp.int32, blocks)
    scale = 1.0 / (1.0 - math.exp(-4.0))
    below = jnp.mod(me - other - 1, blocks).astype(jnp.float32)
    above = jnp.mod(other - me - 1, blocks).astype(jnp.float32)
    return scale * jnp.exp(-step * jnp.stack([below, above]))


def unit(decay):
    ratio = math.exp(-decay)
    return (1.0 - ratio) / (1.0 + ratio)


def shards(fields, residual, past_fields, past_residuals):
    history = past_residuals.shape[0]
    species, height_cells, width_cells, line_cells = residual.shape
    height_total = height_cells * lax.axis_size("gz")
    width_total = width_cells * lax.axis_size("gy")
    cell_total = height_total * width_total * line_cells
    decay_z, decay_y = 4.0 / height_total, 4.0 / width_total
    lines = species * height_cells * width_cells
    f32 = jnp.float32

    rows = min(256, lines)
    size = -(-(history + 1) // 2) * 16
    local = pl.pallas_call(
        functools.partial(gram_kernel, history),
        grid=(lines // rows,),
        in_specs=[
            pl.BlockSpec((history, rows, line_cells), lambda i: (0, i, 0)),
            pl.BlockSpec((rows, line_cells), lambda i: (i, 0)),
            pl.BlockSpec((rows, line_cells), lambda i: (i, 0)),
        ],
        out_specs=pl.BlockSpec((32, 128), lambda i: (0, 0)),
        out_shape=jax.ShapeDtypeStruct((32, 128), f32),
        scratch_shapes=[
            pltpu.VMEM((size, rows // 8 * 128), jnp.bfloat16),
            pltpu.VMEM((size, rows // 8 * 128), jnp.bfloat16),
            pltpu.VMEM((2, size, size), f32),
            pltpu.VMEM((8, 128), f32),
        ],
        compiler_params=params(1),
        name="gram",
    )(
        past_residuals.reshape(history, lines, line_cells),
        residual.reshape(lines, line_cells),
        fields.reshape(lines, line_cells),
    )
    parts = lax.all_gather(local, ("gz", "gy"), axis=0, tiled=False)

    planes = 2 if height_cells % 2 == 0 else 1
    slab = (1, planes, width_cells, line_cells)
    slab_map = lambda s, z: (s, z, 0, 0)
    grid_shape = jax.ShapeDtypeStruct(residual.shape, f32)
    base, mixed, ends, stats = pl.pallas_call(
        functools.partial(mix_kernel, history, decay_z),
        grid=(species, height_cells // planes),
        in_specs=[
            pl.BlockSpec(parts.shape, lambda s, z: (0, 0, 0)),
            pl.BlockSpec((history, *slab), lambda s, z: (0, s, z, 0, 0)),
            pl.BlockSpec((history, *slab), lambda s, z: (0, s, z, 0, 0)),
            pl.BlockSpec(slab, slab_map),
            pl.BlockSpec(slab, slab_map),
        ],
        out_specs=[
            pl.BlockSpec(slab, slab_map),
            pl.BlockSpec(slab, slab_map),
            pl.BlockSpec((1, 2, width_cells, line_cells), lambda s, z: (s, 0, 0, 0)),
            pl.BlockSpec((16, 128), lambda s, z: (0, 0)),
        ],
        out_shape=[
            grid_shape,
            grid_shape,
            jax.ShapeDtypeStruct((species, 2, width_cells, line_cells), f32),
            jax.ShapeDtypeStruct((16, 128), f32),
        ],
        scratch_shapes=[pltpu.VMEM((24, 128), f32)],
        compiler_params=params(2),
        name="mix",
    )(parts, past_fields, past_residuals, fields, residual)
    every_end = lax.all_gather(ends, "gz", axis=0, tiled=False)

    ratio = math.exp(-decay_y)
    offset = np.arange(width_cells)
    taps = np.zeros((width_cells + 8, width_cells))
    taps[:width_cells] = ratio ** np.abs(offset[:, None] - offset[None, :])
    taps[width_cells] = ratio ** (width_cells - 1 - offset)
    taps[width_cells + 1] = ratio ** offset
    taps = jnp.asarray(taps * unit(decay_y) * unit(decay_z), f32)
    whole = pl.BlockSpec((1, height_cells, width_cells, line_cells), lambda s: (s, 0, 0, 0))
    partial, tops = pl.pallas_call(
        functools.partial(smooth_kernel, decay_z),
        grid=(species,),
        in_specs=[
            pl.BlockSpec(memory_space=pltpu.SMEM),
            pl.BlockSpec(
                (every_end.shape[0], 1, 2, width_cells, line_cells), lambda s: (0, s, 0, 0, 0)
            ),
            pl.BlockSpec(taps.shape, lambda s: (0, 0)),
            whole,
            whole,
        ],
        out_specs=[
            whole,
            pl.BlockSpec((1, 2, height_cells, line_cells), lambda s: (s, 0, 0, 0)),
        ],
        out_shape=[
            grid_shape,
            jax.ShapeDtypeStruct((species, 2, height_cells, line_cells), f32),
        ],
        scratch_shapes=[pltpu.VMEM((height_cells, width_cells, line_cells), f32)],
        compiler_params=params(1),
        name="smooth",
    )(carry_weights("gz", height_cells, height_total), every_end, taps, mixed, base)
    every_top = lax.all_gather(tops, "gy", axis=0, tiled=False)

    chunk = 8
    both = pl.BlockSpec((species, chunk, width_cells, line_cells), lambda z: (0, z, 0, 0))
    new_fields, energy = pl.pallas_call(
        functools.partial(finish_kernel, decay_y),
        grid=(height_cells // chunk,),
        in_specs=[
            pl.BlockSpec(memory_space=pltpu.SMEM),
            pl.BlockSpec(
                (every_top.shape[0], species, 2, chunk, line_cells), lambda z: (0, 0, 0, z, 0)
            ),
            both,
        ],
        out_specs=[both, pl.BlockSpec((8, 128), lambda z: (0, 0))],
        out_shape=[grid_shape, jax.ShapeDtypeStruct((8, 128), f32)],
        compiler_params=params(1),
        name="finish",
    )(carry_weights("gy", width_cells, width_total), every_top, partial)

    pairs = lax.all_gather(
        jnp.concatenate([energy, stats], axis=0), ("gz", "gy"), axis=0, tiled=False
    )
    summary = jnp.stack(
        [jnp.sum(pairs[:, 0:8]) / cell_total, pairs[0, 16, 0], jnp.max(pairs[:, 8:16])]
    )
    return (new_fields, summary)


def solution(mesh):
    placed = (
        P(None, "gz", "gy", None),
        P(None, "gz", "gy", None),
        P(None, None, "gz", "gy", None),
        P(None, None, "gz", "gy", None),
    )
    return jax.shard_map(
        shards,
        mesh=mesh,
        in_specs=placed,
        out_specs=(P(None, "gz", "gy", None), P()),
        check_vma=False,
    )
```

time: 588 us -> 224 us (0.38); the launches traced: 578 us -> 224 us
  matrix products: 351 us -> 0 us
  Pallas kernels: 0 us -> 74.3 us
  other arithmetic: 44.7 us -> 4.3 us
  blocking collectives: 123 us -> 94.4 us
    dot_general x8 -> x0, matrix products: 350 us -> none  [the longest x1 110 us: shards(): jnp.dot(deltas, deltas.T, precision=EXACT, preferred_element_type=jnp.flo...]
    all_gather x0 -> x3, blocking collectives: none -> 94.4 us  [the longest x1 47.6 us: shards(): parts = lax.all_gather(local, ('gz', 'gy'), axis=0, tiled=False)]
    psum x2 -> x0, blocking collectives: 83.9 us -> none  [the longest x1 42.1 us: shards(): lax.psum((gram_local, intersect_local), ('gz', 'gy'))]
    pallas_call x0 -> x4, Pallas kernels: none -> 74.3 us  [the longest x1 37.9 us: shards(): pl.pallas_call(functools.partial(mix_kernel, history, decay_z), grid=(spe...]
    pmax x1 -> x0, blocking collectives: 39.2 us -> none  [shards(): largest = lax.pmax(peak_local, ('gz', 'gy'))]
    sub x1 -> x0, other arithmetic: 32.5 us -> none  [shards(): deltas = flat_residual[None, :] - past_rows]
    all_gather x2 -> x1, waiting for transfers between devices: 38.6 us -> 35.3 us  [shards(): every_end = lax.all_gather(ends, 'gz', axis=0, tiled=False)]
  transfers between devices with their start and end apart: 2 -> 1, of which waited for: 1 -> 1; matrix products, arithmetic and copies ran while one was open for 12% -> 1% of each run, Pallas kernels for 0% -> 0%
where the time goes in v1:
time: 224 us
  blocking collectives  94.4 us (42%)
  Pallas kernels  74.3 us (33%)
  waiting for transfers between devices  35.4 us (16%)
  between operations  14.7 us (7%)
  other arithmetic  4.3 us (2%)
    all_gather x1, blocking collectives, shards(): parts = lax.all_gather(local, ('gz', 'gy'), axis=0, tiled=False)  47.6 us
    all_gather x1, blocking collectives, shards(): lax.all_gather(jnp.concatenate([energy, stats], axis=0), ('gz', 'gy'), ax...  39.3 us
    pallas_call x1, Pallas kernels, shards(): pl.pallas_call(functools.partial(mix_kernel, history, decay_z), grid=(spe...  37.9 us
    all_gather x1, waiting for transfers between devices, shards(): every_end = lax.all_gather(ends, 'gz', axis=0, tiled=False)  35.3 us
    pallas_call x1, Pallas kernels, shards(): pl.pallas_call(functools.partial(gram_kernel, history), grid=(lines // ro...  25.2 us
    all_gather x1, blocking collectives, shards(): every_top = lax.all_gather(tops, 'gy', axis=0, tiled=False)  7.49 us
    pallas_call x1, Pallas kernels, shards(): pl.pallas_call(functools.partial(smooth_kernel, decay_z), grid=(species,)...  7 us
  transfers between devices with their start and end apart: 1, of which 1 were waited for; matrix products, arithmetic and copies ran while one was open for 1% of the time, Pallas kernels for 0%

profile of v1, /device:TPU:0, one launch (start us, length us, event | category | flops | bytes accessed | tf_op | source)
XLA Modules:
  0.0 223.5 jit_solution(1541852574400199091)
XLA Ops:
  7.2 0.0 all-gather.6.cloned.1.call-start
  7.2 25.2 %gram.1 = f32[32,128]{1,0:T(8,128)} custom-call(f32[20,4096,128]{2,1,0:T(8,128)} %bitcast.10, f32[4096,128]{1,0:T(8,128)} %bitcast.11, f32[4096,128]{1,0:T(8,128)} %bitcast.12), custom_call_target="tpu_custom_call" | custom-call | tf_op jit(solution)/shard_map/gram/pallas_call | solution.py:230
  32.5 47.6 %all-gather = f32[1024,128]{1,0:T(8,128)} all-gather(f32[32,128]{1,0:T(8,128)} %gram.1), channel_id=2, replica_groups=mesh['gz'=8,'gy'=4] {'gz','gy'}, dimensions={0}, use_global_device_ids=true | all-gather | bytes 540672 | tf_op jit(solution)/shard_map/all_gather | solution.py:253
  80.0 37.9 %mix.1 = (f32[2,32,64,128]{3,2,1,0:T(8,128)}, f32[2,32,64,128]{3,2,1,0:T(8,128)}, f32[2,2,64,128]{3,2,1,0:T(8,128)}, f32[16,128]{1,0:T(8,128)}) custom-call(f32[32,32,128]{2,1,0:T(8,128)} %bitcast.13, f32[20,2,32,64,128]{4,3,2,1,0:T(8,128)} %pf_ref.1, f32[20,2,32,64,128]{4,3,2,1,0:T(8,128)} %pr_ref.1, f32[2,32,64,128]{3,2,1,0:T(8,128)} %field_ref.1, ...), custom_call_target="tpu_custom_call" | custom-call | tf_op jit(solution)/shard_map/mix/pallas_call | solution.py:259
  117.9 0.0 all-gather.6.cloned.1.call-update
  118.0 0.6 fusion.3.weight_ref
  118.6 0.6 fusion.1.weight_ref
  119.2 35.3 %all-gather.6.cloned.1.call-done = f32[16,2,64,128]{3,2,1,0:T(8,128)} async-done(((f32[2,2,64,128]{3,2,1,0:T(8,128)}), f32[16,2,64,128]{3,2,1,0:T(8,128)}) %all-gather.6.cloned.1.call-update) | async-done | bytes 1048592 | tf_op jit(solution)/shard_map/all_gather | solution.py:285
  154.5 7.0 %smooth.1 = (f32[2,32,64,128]{3,2,1,0:T(8,128)}, f32[2,2,32,128]{3,2,1,0:T(8,128)}) custom-call(f32[2,8]{1,0:T(2,128)} %fusion.3.weight_ref, f32[8,2,2,64,128]{4,3,2,1,0:T(8,128)} %bitcast.16, f32[72,64]{1,0:T(8,128)} %constant.71.clone.taps_ref, f32[2,32,64,128]{3,2,1,0:T(8,128)} %get-tuple-element.11.mixed_ref, f32[2,32,64,128]{3,2,1,0:T(8,128)} %get-tuple-element.12.base_ref), custom_call_target="tpu_custom_call" | custom-call | tf_op jit(solution)/shard_map/smooth/pallas_call | solution.py:295
  161.5 0.0 copy-start
  161.5 7.5 %all-gather.2 = f32[8,2,32,128]{3,2,1,0:T(8,128)} all-gather(f32[2,2,32,128]{3,2,1,0:T(8,128)} %get-tuple-element.13), channel_id=4, replica_groups=mesh['gz'=8,'gy'=4] {'gy'}, dimensions={0}, use_global_device_ids=true | all-gather | bytes 327680 | tf_op jit(solution)/shard_map/all_gather | solution.py:319
  169.0 4.1 %finish.1 = (f32[2,32,64,128]{3,2,1,0:T(8,128)}, f32[8,128]{1,0:T(8,128)}) custom-call(f32[2,4]{1,0:T(2,128)} %fusion.1.weight_ref, f32[4,2,2,32,128]{4,3,2,1,0:T(8,128)} %bitcast.17, f32[2,32,64,128]{3,2,1,0:T(8,128)} %get-tuple-element.14.part_ref), custom_call_target="tpu_custom_call" | custom-call | tf_op jit(solution)/shard_map/finish/pallas_call | solution.py:323
  173.1 0.0 copy-done
  173.1 0.7 pad_maximum_fusion
  173.8 39.3 %all-gather.3 = f32[768,128]{1,0:T(8,128)S(1)} all-gather(f32[24,128]{1,0:T(8,128)S(1)} %pad_maximum_fusion), channel_id=5, replica_groups=mesh['gz'=8,'gy'=4] {'gz','gy'}, dimensions={0}, use_global_device_ids=true | all-gather | bytes 405504 | tf_op jit(solution)/shard_map/all_gather | solution.py:339
  213.1 0.6 slice_reduce_fusion.1
  213.8 0.5 slice.13
  214.9 1.8 pad_maximum_fusion.1
  (2 shorter events, 0.0 us)
Async XLA Ops:
  7.2 147.3 %all-gather.6.cloned.1.call-start = ((), (), s32[]{:S(2)}) async-start(), calls=%async_computation | async-start | bytes 1179648 | tf_op jit(solution)/shard_map/all_gather | solution.py:285
  161.5 11.6 %copy-start = (f32[16,128]{1,0:T(8,128)S(1)}, f32[16,128]{1,0:T(8,128)}, u32[]{:S(2)}) copy-start(f32[16,128]{1,0:T(8,128)} %get-tuple-element.17) | copy-start | bytes 24580
Sparse Core Ops, SparseCore 0:
  118.1 36.3 all-gather.5
